TPU v7x, 32 devices: a whole 2x2x4 slice. The times are simulated.
32 devices in a mesh: dp: 4 (over z), seq: 8 (over y, x, core).
Axes of the slice: x: 2, y: 2, z: 4, core: 2. Of those that a mesh axis runs over, the one named last changes fastest.
Arguments:
- layer_input: bfloat16 [4, 2048, 1152], P('dp', 'seq'), may hold values from -6 to 6
- segment_ids: int32 [4, 2048], P('dp'), may hold values from 0 to 3, as said below
- position_ids: int32 [4, 2048], P('dp', 'seq'), may hold values from 0 to 1023, as said below
- w_query: bfloat16 [1152, 1024], P('seq'), may hold values from -0.1875 to 0.1875
- w_keyval: bfloat16 [1152, 512], P('seq'), may hold values from -0.1875 to 0.1875
- w_out: bfloat16 [1024, 1152], P('seq'), may hold values from -0.1875 to 0.1875
- w_gate: bfloat16 [1152, 6912], P(None, 'seq'), may hold values from -0.1875 to 0.1875
- w_up: bfloat16 [1152, 6912], P(None, 'seq'), may hold values from -0.1875 to 0.1875
- w_down: bfloat16 [6912, 1152], P('seq'), may hold values from -0.078125 to 0.078125
- g_input: float32 [1152], replicated, may hold values from 0.25 to 1.75
- g_post_attn: float32 [1152], replicated, may hold values from 0.25 to 1.75
- g_pre_ffn: float32 [1152], replicated, may hold values from 0.25 to 1.75
- g_post_ffn: float32 [1152], replicated, may hold values from 0.25 to 1.75
- g_query: float32 [256], replicated, may hold values from 0.25 to 1.75
- g_key: float32 [256], replicated, may hold values from 0.25 to 1.75
- out_grad: float32 [4, 2048, 1152], P('dp', 'seq'), may hold values from -6 to 6
Outputs:
- layer_output: bfloat16 [4, 2048, 1152], P('dp', 'seq')
- input_grad: float32 [4, 2048, 1152], P('dp', 'seq')
- grad_w_query: float32 [1152, 1024], P('seq')
- grad_w_keyval: float32 [1152, 512], P('seq')
- grad_w_out: float32 [1024, 1152], P('seq')
- grad_w_gate: float32 [1152, 6912], P(None, 'seq')
- grad_w_up: float32 [1152, 6912], P(None, 'seq')
- grad_w_down: float32 [6912, 1152], P('seq')
- grad_g_input: float32 [1152], P('seq')
- grad_g_post_attn: float32 [1152], P('seq')
- grad_g_pre_ffn: float32 [1152], P('seq')
- grad_g_post_ffn: float32 [1152], P('seq')
- grad_g_query: float32 [256], P('seq')
- grad_g_key: float32 [256], P('seq')
Inputs may be any that keep to these rules, and one draw needn't show every extreme that they name: `segment_ids`: in each row the ids never fall, start at 0 and rise by one at each document's first token; every row holds 4 documents, none longer than 1024 tokens, and in every row one of them is exactly that long. `position_ids`: A token's place within its document: 0 at the document's first token, rising by one along it; the documents are those of segment_ids.
All inputs are finite; a program needn't handle non-finite values.
Results may differ from a plain program's by a relative error of at most 0.023.
Values may be sent and summed in bfloat16 or wider, within the bound.
No kernel may reach another device: no remote copies, remote signals or barrier semaphores. Data moves between devices by JAX's collectives and lax.ppermute only.
A program may use at most 256 MiB of HBM per device.

v0:
```python
import jax
import jax.numpy as jnp
from jax import lax
from jax.sharding import PartitionSpec as P

HEADS = 4
HEAD = 256
norm_eps = 1e-06
rope_base = 1000000.0


def rms_forward(values):
    factor = lax.rsqrt(jnp.mean(values * values, axis=-1, keepdims=True) + norm_eps)
    return (values * factor, factor)


def rms_backward(upstream, normed, factor):
    return factor * (upstream - normed * jnp.mean(upstream * normed, axis=-1, keepdims=True))


def rope_angles(positions, width):
    half_width = width // 2
    inverse_freq = rope_base ** (-(jnp.arange(half_width).astype(jnp.float32) * 2.0 / width))
    return positions.astype(jnp.float32)[:, None] * inverse_freq[None, :]


def rotate(values, angles):
    half_width = values.shape[-1] // 2
    first_half = values[..., :half_width]
    second_half = values[..., half_width:]
    cosine = jnp.cos(angles)
    sine_part = jnp.sin(angles)
    return jnp.concatenate(
        [
            first_half * cosine - second_half * sine_part,
            second_half * cosine + first_half * sine_part,
        ],
        axis=-1,
    )


def dot_rows(left, right):
    return lax.dot_general(
        left, right, (((1,), (1,)), ((), ())), preferred_element_type=jnp.float32
    )


def dot_cols(left, right):
    return lax.dot_general(
        left, right, (((0,), (0,)), ((), ())), preferred_element_type=jnp.float32
    )


def gelu_gate(gate_proj, up_proj):
    return jax.nn.gelu(gate_proj, approximate=True) * up_proj


def on_device(
    layer_input,
    segment_ids,
    position_ids,
    w_query,
    w_keyval,
    w_out,
    w_gate,
    w_up,
    w_down,
    g_input,
    g_post_attn,
    g_pre_ffn,
    g_post_ffn,
    g_query,
    g_key,
    out_grad,
):
    local_rows = layer_input.shape[1]
    row_len = local_rows * lax.axis_size("seq")
    row_offset = lax.axis_index("seq") * local_rows
    input_f32 = layer_input[0].astype(jnp.float32)
    seg_row = segment_ids[0]
    seg_local = lax.dynamic_slice_in_dim(seg_row, row_offset, local_rows)
    angles = rope_angles(position_ids[0], HEAD)
    score_scale = HEAD ** (-0.5)
    query_full, keyval_full, out_full, gate_full, up_full, down_full = (
        lax.all_gather(w_query, "seq", axis=0, tiled=True),
        lax.all_gather(w_keyval, "seq", axis=0, tiled=True),
        lax.all_gather(w_out, "seq", axis=0, tiled=True),
        lax.all_gather(w_gate, "seq", axis=1, tiled=True),
        lax.all_gather(w_up, "seq", axis=1, tiled=True),
        lax.all_gather(w_down, "seq", axis=0, tiled=True),
    )
    a_normed, a_factor = rms_forward(input_f32)
    a_low = (a_normed * g_input).astype(jnp.bfloat16)
    q_pre = jnp.dot(a_low, query_full, preferred_element_type=jnp.float32).reshape(
        local_rows, HEADS, HEAD
    )
    kv_pre = jnp.dot(a_low, keyval_full, preferred_element_type=jnp.float32)
    q_hat, q_factor = rms_forward(q_pre)
    q_low = rotate(q_hat * g_query, angles[:, None, :]).astype(jnp.bfloat16)
    k_hat, k_factor = rms_forward(kv_pre[:, :HEAD])
    k_low = rotate(k_hat * g_key, angles).astype(jnp.bfloat16)
    kv_low = jnp.concatenate([k_low, kv_pre[:, HEAD:].astype(jnp.bfloat16)], axis=1)
    kv_row = lax.all_gather(kv_low, "seq", axis=0, tiled=True)
    key_block = min(512, row_len)
    first_block = jnp.maximum(row_offset - row_len // 2 + 1, 0) // key_block
    end_block = (row_offset + local_rows - 1) // key_block + 1
    query_rows = q_low.reshape(local_rows * HEADS, HEAD)
    query_index = jnp.broadcast_to(
        (row_offset + jnp.arange(local_rows, dtype=jnp.int32))[:, None], (local_rows, HEADS)
    ).reshape(-1)
    query_seg = jnp.broadcast_to(seg_local[:, None], (local_rows, HEADS)).reshape(-1)

    def block_at(block_num):
        key_start = (block_num * key_block).astype(jnp.int32)
        kv_piece = lax.dynamic_slice_in_dim(kv_row, key_start, key_block, 0)
        seg_piece = lax.dynamic_slice_in_dim(seg_row, key_start, key_block, 0)
        return (key_start, kv_piece, seg_piece)

    def block_scores(key_start, key_rows, key_seg):
        raw_scores = dot_rows(query_rows, key_rows) * score_scale
        key_index = key_start + jnp.arange(key_block, dtype=jnp.int32)
        visible = (key_seg[None, :] == query_seg[:, None]) & (
            key_index[None, :] <= query_index[:, None]
        )
        return (raw_scores, visible)

    def max_and_total(block_num, state_pair):
        row_max, exp_total = state_pair
        key_start, kv_piece, seg_piece = block_at(block_num)
        raw_scores, visible = block_scores(key_start, kv_piece[:, :HEAD], seg_piece)
        masked = jnp.where(visible, raw_scores, -1e30)
        new_max = jnp.maximum(row_max, jnp.max(masked, axis=1))
        shifted = jnp.where(visible, jnp.exp(masked - new_max[:, None]), 0.0)
        exp_total = exp_total * jnp.exp(row_max - new_max) + jnp.sum(shifted, axis=1)
        return (new_max, exp_total)

    start_max = jnp.full((local_rows * HEADS,), -1e30, jnp.float32)
    start_total = jnp.zeros((local_rows * HEADS,), jnp.float32)
    row_max, exp_total = lax.fori_loop(
        first_block, end_block, max_and_total, (start_max, start_total)
    )
    log_total = row_max + jnp.log(exp_total)

    def weighted_sum(block_num, accum):
        key_start, kv_piece, seg_piece = block_at(block_num)
        raw_scores, visible = block_scores(key_start, kv_piece[:, :HEAD], seg_piece)
        attn_prob = jnp.where(visible, jnp.exp(raw_scores - log_total[:, None]), 0.0).astype(
            jnp.bfloat16
        )
        return accum + jnp.dot(attn_prob, kv_piece[:, HEAD:], preferred_element_type=jnp.float32)

    attended_rows = lax.fori_loop(
        first_block, end_block, weighted_sum, jnp.zeros((local_rows * HEADS, HEAD), jnp.float32)
    )
    attended_low = attended_rows.reshape(local_rows, HEADS * HEAD).astype(jnp.bfloat16)
    attn_proj = jnp.dot(attended_low, out_full, preferred_element_type=jnp.float32)
    attn_normed, attn_factor = rms_forward(attn_proj)
    middle = input_f32 + attn_normed * g_post_attn
    b_normed, b_factor = rms_forward(middle)
    b_low = (b_normed * g_pre_ffn).astype(jnp.bfloat16)
    gate_proj = jnp.dot(b_low, gate_full, preferred_element_type=jnp.float32)
    up_proj = jnp.dot(b_low, up_full, preferred_element_type=jnp.float32)
    hidden_low = gelu_gate(gate_proj, up_proj).astype(jnp.bfloat16)
    ffn_out = jnp.dot(hidden_low, down_full, preferred_element_type=jnp.float32)
    ffn_normed, ffn_factor = rms_forward(ffn_out)
    layer_out = (middle + ffn_normed * g_post_ffn).astype(jnp.bfloat16)
    grad_top = out_grad[0]
    gain_post_ffn = jnp.sum(grad_top * ffn_normed, axis=0)
    d_ffn_low = rms_backward(grad_top * g_post_ffn, ffn_normed, ffn_factor).astype(jnp.bfloat16)
    d_hidden = dot_rows(d_ffn_low, down_full)
    grad_down = dot_cols(hidden_low, d_ffn_low)
    _, gelu_back = jax.vjp(gelu_gate, gate_proj, up_proj)
    d_gate, d_up = gelu_back(d_hidden)
    d_gate_low = d_gate.astype(jnp.bfloat16)
    d_up_low = d_up.astype(jnp.bfloat16)
    grad_gate = dot_cols(b_low, d_gate_low)
    grad_upw = dot_cols(b_low, d_up_low)
    d_b = dot_rows(d_gate_low, gate_full) + dot_rows(d_up_low, up_full)
    gain_pre_ffn = jnp.sum(d_b * b_normed, axis=0)
    d_middle = grad_top + rms_backward(d_b * g_pre_ffn, b_normed, b_factor)
    gain_post_attn = jnp.sum(d_middle * attn_normed, axis=0)
    d_attn_low = rms_backward(d_middle * g_post_attn, attn_normed, attn_factor).astype(jnp.bfloat16)
    grad_outw = dot_cols(attended_low, d_attn_low)
    d_attended = dot_rows(d_attn_low, out_full).astype(jnp.bfloat16)
    d_attended_rows = d_attended.reshape(local_rows * HEADS, HEAD)
    row_dot = jnp.sum(d_attended_rows.astype(jnp.float32) * attended_rows, axis=1)

    def attend_back(block_num, carry):
        d_query, d_kv_whole = carry
        key_start, kv_piece, seg_piece = block_at(block_num)
        raw_scores, visible = block_scores(key_start, kv_piece[:, :HEAD], seg_piece)
        attn_prob = jnp.where(visible, jnp.exp(raw_scores - log_total[:, None]), 0.0)
        prob_low = attn_prob.astype(jnp.bfloat16)
        d_prob = dot_rows(d_attended_rows, kv_piece[:, HEAD:])
        d_scores = (attn_prob * (d_prob - row_dot[:, None])).astype(jnp.bfloat16)
        d_query = (
            d_query
            + jnp.dot(d_scores, kv_piece[:, :HEAD], preferred_element_type=jnp.float32)
            * score_scale
        )
        d_keys = dot_cols(d_scores, query_rows) * score_scale
        d_values = dot_cols(prob_low, d_attended_rows)
        d_kv_whole = lax.dynamic_update_slice_in_dim(
            d_kv_whole, jnp.concatenate([d_keys, d_values], axis=1), key_start, 0
        )
        return (d_query, d_kv_whole)

    d_query, d_kv_whole = lax.fori_loop(
        first_block,
        end_block,
        attend_back,
        (
            jnp.zeros((local_rows * HEADS, HEAD), jnp.float32),
            jnp.zeros((row_len, 2 * HEAD), jnp.float32),
        ),
    )
    d_kv = lax.psum_scatter(
        d_kv_whole.astype(jnp.bfloat16), "seq", scatter_dimension=0, tiled=True
    ).astype(jnp.float32)
    d_q_normed = rotate(d_query.reshape(local_rows, HEADS, HEAD), -angles[:, None, :])
    gain_query = jnp.sum(d_q_normed * q_hat, axis=(0, 1))
    d_q_pre = (
        rms_backward(d_q_normed * g_query, q_hat, q_factor)
        .reshape(local_rows, HEADS * HEAD)
        .astype(jnp.bfloat16)
    )
    d_k_normed = rotate(d_kv[:, :HEAD], -angles)
    gain_key = jnp.sum(d_k_normed * k_hat, axis=0)
    d_k_pre = rms_backward(d_k_normed * g_key, k_hat, k_factor)
    d_kv_low = jnp.concatenate([d_k_pre, d_kv[:, HEAD:]], axis=1).astype(jnp.bfloat16)
    grad_queryw = dot_cols(a_low, d_q_pre)
    grad_keyvalw = dot_cols(a_low, d_kv_low)
    d_a = dot_rows(d_q_pre, query_full) + dot_rows(d_kv_low, keyval_full)
    gain_input = jnp.sum(d_a * a_normed, axis=0)
    d_input = d_middle + rms_backward(d_a * g_input, a_normed, a_factor)
    (
        grad_queryw,
        grad_keyvalw,
        grad_outw,
        grad_gate,
        grad_upw,
        grad_down,
        gain_input,
        gain_post_attn,
        gain_pre_ffn,
        gain_post_ffn,
        gain_query,
        gain_key,
    ) = (
        lax.psum_scatter(
            grad_queryw.astype(jnp.bfloat16), "seq", scatter_dimension=0, tiled=True
        ).astype(jnp.float32),
        lax.psum_scatter(
            grad_keyvalw.astype(jnp.bfloat16), "seq", scatter_dimension=0, tiled=True
        ).astype(jnp.float32),
        lax.psum_scatter(
            grad_outw.astype(jnp.bfloat16), "seq", scatter_dimension=0, tiled=True
        ).astype(jnp.float32),
        lax.psum_scatter(
            grad_gate.astype(jnp.bfloat16), "seq", scatter_dimension=1, tiled=True
        ).astype(jnp.float32),
        lax.psum_scatter(
            grad_upw.astype(jnp.bfloat16), "seq", scatter_dimension=1, tiled=True
        ).astype(jnp.float32),
        lax.psum_scatter(
            grad_down.astype(jnp.bfloat16), "seq", scatter_dimension=0, tiled=True
        ).astype(jnp.float32),
        lax.psum_scatter(
            gain_input.astype(jnp.bfloat16), "seq", scatter_dimension=0, tiled=True
        ).astype(jnp.float32),
        lax.psum_scatter(
            gain_post_attn.astype(jnp.bfloat16), "seq", scatter_dimension=0, tiled=True
        ).astype(jnp.float32),
        lax.psum_scatter(
            gain_pre_ffn.astype(jnp.bfloat16), "seq", scatter_dimension=0, tiled=True
        ).astype(jnp.float32),
        lax.psum_scatter(
            gain_post_ffn.astype(jnp.bfloat16), "seq", scatter_dimension=0, tiled=True
        ).astype(jnp.float32),
        lax.psum_scatter(
            gain_query.astype(jnp.bfloat16), "seq", scatter_dimension=0, tiled=True
        ).astype(jnp.float32),
        lax.psum_scatter(
            gain_key.astype(jnp.bfloat16), "seq", scatter_dimension=0, tiled=True
        ).astype(jnp.float32),
    )
    totals = (
        lax.psum(grad_queryw.astype(jnp.bfloat16), "dp").astype(jnp.float32),
        lax.psum(grad_keyvalw.astype(jnp.bfloat16), "dp").astype(jnp.float32),
        lax.psum(grad_outw.astype(jnp.bfloat16), "dp").astype(jnp.float32),
        lax.psum(grad_gate.astype(jnp.bfloat16), "dp").astype(jnp.float32),
        lax.psum(grad_upw.astype(jnp.bfloat16), "dp").astype(jnp.float32),
        lax.psum(grad_down.astype(jnp.bfloat16), "dp").astype(jnp.float32),
        lax.psum(gain_input.astype(jnp.bfloat16), "dp").astype(jnp.float32),
        lax.psum(gain_post_attn.astype(jnp.bfloat16), "dp").astype(jnp.float32),
        lax.psum(gain_pre_ffn.astype(jnp.bfloat16), "dp").astype(jnp.float32),
        lax.psum(gain_post_ffn.astype(jnp.bfloat16), "dp").astype(jnp.float32),
        lax.psum(gain_query.astype(jnp.bfloat16), "dp").astype(jnp.float32),
        lax.psum(gain_key.astype(jnp.bfloat16), "dp").astype(jnp.float32),
    )
    return (
        layer_out[None],
        d_input[None],
        totals[0],
        totals[1],
        totals[2],
        totals[3],
        totals[4],
        totals[5],
        totals[6],
        totals[7],
        totals[8],
        totals[9],
        totals[10],
        totals[11],
    )


def solution(mesh):
    in_specs = (
        P("dp", "seq", None),
        P("dp", None),
        P("dp", "seq"),
        P("seq", None),
        P("seq", None),
        P("seq", None),
        P(None, "seq"),
        P(None, "seq"),
        P("seq", None),
        P(),
        P(),
        P(),
        P(),
        P(),
        P(),
        P("dp", "seq", None),
    )
    out_specs = (
        P("dp", "seq", None),
        P("dp", "seq", None),
        P("seq", None),
        P("seq", None),
        P("seq", None),
        P(None, "seq"),
        P(None, "seq"),
        P("seq", None),
        P("seq"),
        P("seq"),
        P("seq"),
        P("seq"),
        P("seq"),
        P("seq"),
    )
    return jax.shard_map(
        on_device, mesh=mesh, in_specs=in_specs, out_specs=out_specs, check_vma=False
    )
```

profile of v0, /device:TPU:0, one launch (start us, length us, event | category | flops | bytes accessed | tf_op | source)
XLA Modules:
  0.0 1255.0 jit_solution(4688408701022514957)
XLA Ops:
  10.7 26.0 %all-gather.8.cloned.1.call-done = bf16[1152,512]{1,0:T(8,128)(2,1)} async-done(((bf16[144,512]{1,0:T(8,128)(2,1)}), bf16[1152,512]{1,0:T(8,128)(2,1)}) %all-gather.8.cloned.1.call-update) | async-done | bytes 1179664 | tf_op jit(solution)/shard_map/all_gather | solution.py:86
  44.8 22.8 %all-gather.12.cloned.1.call-done = bf16[1152,1024]{1,0:T(8,128)(2,1)} async-done(((bf16[144,1024]{1,0:T(8,128)(2,1)}), bf16[1152,1024]{1,0:T(8,128)(2,1)}) %all-gather.12.cloned.1.call-update) | async-done | bytes 2359312 | tf_op jit(solution)/shard_map/all_gather | solution.py:85
  67.6 3.1 copy.39
  73.0 25.0 %all-gather.10.cloned.1.call-done = bf16[2048,512]{1,0:T(8,128)(2,1)} async-done(((bf16[256,512]{1,0:T(8,128)(2,1)}), bf16[2048,512]{1,0:T(8,128)(2,1)}) %all-gather.10.cloned.1.call-update) | async-done | bytes 2097168 | tf_op jit(solution)/shard_map/all_gather | solution.py:103
  98.0 2.9 while.37
  101.0 2.8 while.38
  104.8 24.0 %all-gather.14.cloned.1.call-done = bf16[1024,1152]{1,0:T(8,128)(2,1)} async-done(((bf16[128,1152]{1,0:T(8,128)(2,1)}), bf16[1024,1152]{1,0:T(8,128)(2,1)}) %all-gather.14.cloned.1.call-update) | async-done | bytes 2359312 | tf_op jit(solution)/shard_map/all_gather | solution.py:87
  128.8 2.7 multiply_reduce_fusion.7
  132.4 84.5 %all-gather.16.cloned.1.call-done = bf16[1152,6912]{0,1:T(8,128)(2,1)} async-done(((bf16[1152,864]{0,1:T(8,128)(2,1)}), bf16[1152,6912]{0,1:T(8,128)(2,1)}) %all-gather.16.cloned.1.call-update) | async-done | bytes 15925264 | tf_op jit(solution)/shard_map/all_gather | solution.py:88
  216.9 16.5 %fusion.84 = f32[256,6912]{1,0:T(8,128)} fusion(bf16[256,1152]{1,0:T(8,128)(2,1)S(1)} %multiply_convert_fusion.4, bf16[1152,6912]{0,1:T(8,128)(2,1)} %all-gather.16.cloned.1.call-done), kind=kOutput, calls=%fused_computation.160 | convolution fusion | flops 4076863488 | bytes 23592960 | tf_op jit(solution)/shard_map/dot_general | solution.py:161
  233.4 71.5 %all-gather.18.cloned.1.call-done = bf16[1152,6912]{0,1:T(8,128)(2,1)} async-done(((bf16[1152,864]{0,1:T(8,128)(2,1)}), bf16[1152,6912]{0,1:T(8,128)(2,1)}) %all-gather.18.cloned.1.call-update) | async-done | bytes 15925264 | tf_op jit(solution)/shard_map/all_gather | solution.py:89
  304.9 12.7 %multiply_convert_fusion.1 = (bf16[256,6912]{1,0:T(8,128)(2,1)}, f32[256,6912]{1,0:T(8,128)}) fusion(f32[256,6912]{1,0:T(8,128)} %fusion.84, bf16[256,1152]{1,0:T(8,128)(2,1)S(1)} %multiply_convert_fusion.4, bf16[1152,6912]{0,1:T(8,128)(2,1)} %all-gather.18.cloned.1.call-done), kind=kOutput, calls=%fused_computation.61 | convolution fusion | flops 4094558208 | bytes 34209792 | tf_op jit(solution)/shard_map/dot_general | solution.py:162
  317.6 75.5 %all-gather.20.cloned.1.call-done = bf16[6912,1152]{1,0:T(8,128)(2,1)} async-done(((bf16[864,1152]{1,0:T(8,128)(2,1)}), bf16[6912,1152]{1,0:T(8,128)(2,1)}) %all-gather.20.cloned.1.call-update) | async-done | bytes 15925264 | tf_op jit(solution)/shard_map/all_gather | solution.py:90
  393.1 10.5 multiply_reduce_fusion.5
  405.2 16.0 %multiply_convert_fusion = (bf16[256,6912]{1,0:T(8,128)(2,1)}, bf16[256,6912]{1,0:T(8,128)(2,1)}) fusion(f32[256,6912]{1,0:T(8,128)} %fusion.84, f32[256,6912]{1,0:T(8,128)} %get-tuple-element.378, bf16[256,1152]{1,0:T(8,128)(2,1)S(1)} %get-tuple-element.359, bf16[6912,1152]{1,0:T(8,128)(2,1)} %all-gather.20.cloned.1.call-done), kind=kOutput, calls=%fused_computation.60 | convolution fusion | flops 4119330816 | bytes 37748736 | tf_op jit(solution)/shard_map/dot_general | solution.py:43
  421.3 10.5 fusion.85
  431.8 9.5 multiply_reduce_fusion
  448.4 7.5 while.39
  465.0 47.4 %reduce-scatter.8.cloned.1.call-done = bf16[256,512]{1,0:T(8,128)(2,1)} async-done(((bf16[2048,512]{1,0:T(8,128)(2,1)}), bf16[256,512]{1,0:T(8,128)(2,1)}) %reduce-scatter.8.cloned.1.call-update) | async-done | bytes 262160 | tf_op jit(solution)/shard_map/reduce_scatter | solution.py:217
  517.0 10.9 convolution_convert_fusion.2
  528.0 11.0 convolution_convert_fusion.1
  540.1 10.9 convolution_convert_fusion
  551.3 7.4 reduce-scatter.10.cloned.1.call-done
  558.7 45.7 %reduce-scatter.14.cloned.1.call-done = bf16[128,1152]{1,0:T(8,128)(2,1)} async-done(((bf16[1024,1152]{1,0:T(8,128)(2,1)}), bf16[128,1152]{1,0:T(8,128)(2,1)}) %reduce-scatter.14.cloned.1.call-update) | async-done | bytes 294928 | tf_op jit(solution)/shard_map/reduce_scatter | solution.py:256
  604.4 40.4 %reduce-scatter.12.cloned.1.call-done = bf16[144,512]{1,0:T(8,128)(2,1)} async-done(((bf16[1152,512]{1,0:T(8,128)(2,1)}), bf16[144,512]{1,0:T(8,128)(2,1)}) %reduce-scatter.12.cloned.1.call-update) | async-done | bytes 147472 | tf_op jit(solution)/shard_map/reduce_scatter | solution.py:253
  644.8 116.4 %reduce-scatter.16.cloned.1.call-done = bf16[1152,864]{0,1:T(8,128)(2,1)} async-done(((bf16[1152,6912]{0,1:T(8,128)(2,1)}), bf16[1152,864]{0,1:T(8,128)(2,1)}) %reduce-scatter.16.cloned.1.call-update) | async-done | bytes 1990672 | tf_op jit(solution)/shard_map/reduce_scatter | solution.py:259
  761.1 117.0 %reduce-scatter.18.cloned.1.call-done = bf16[1152,864]{0,1:T(8,128)(2,1)} async-done(((bf16[1152,6912]{0,1:T(8,128)(2,1)}), bf16[1152,864]{0,1:T(8,128)(2,1)}) %reduce-scatter.18.cloned.1.call-update) | async-done | bytes 1990672 | tf_op jit(solution)/shard_map/reduce_scatter | solution.py:262
  878.1 116.4 %reduce-scatter.20.cloned.1.call-done = bf16[864,1152]{1,0:T(8,128)(2,1)} async-done(((bf16[6912,1152]{1,0:T(8,128)(2,1)}), bf16[864,1152]{1,0:T(8,128)(2,1)}) %reduce-scatter.20.cloned.1.call-update) | async-done | bytes 1990672 | tf_op jit(solution)/shard_map/reduce_scatter | solution.py:265
  997.6 2.9 fusion.62
  1000.5 24.3 %all-reduce.6 = (bf16[1152]{0:T(1024)(128)(2,1)S(1)}, bf16[1152]{0:T(1024)(128)(2,1)S(1)}, bf16[1152]{0:T(1024)(128)(2,1)S(1)}, bf16[1152]{0:T(1024)(128)(2,1)S(...) all-reduce(bf16[1152]{0:T(1024)(128)(2,1)S(1)} %get-tuple-element.2, ...), channel_id=9, replica_groups=mesh['dp'=4,'seq'=8] {'seq'}, use_global_device_ids=true, to_apply=%region_35.36.clone | all-reduce | flops 5120 | bytes 20480
  1025.2 12.4 all-reduce.7
  1042.3 193.6 %all-reduce.11.cloned.1.call-done = (bf16[144,1024]{1,0:T(8,128)(2,1)}, bf16[144,512]{1,0:T(8,128)(2,1)}, bf16[128,1152]{1,0:T(8,128)(2,1)}, bf16[1152,864]{0,1:...) async-done(((bf16[144,1024]{1,0:T(8,128)(2,1)}, bf16[144,512]{1,0:T(8,128)(2,1)}, bf16[128,1152]{1,0:T(8,128)(2,1)}, bf16[1152,864]{0,1:T(8,128)(2,1)}, ...) | async-done | bytes 6709264 | tf_op jit(solution)/shard_map/psum | solution.py:288
  (243 shorter events, 71.3 us)
Async XLA Ops:
  7.2 32.4 %copy-start.43 = (f32[256]{0:T(256)S(1)}, f32[256]{0:T(256)}, u32[]{:S(2)}) copy-start(f32[256]{0:T(256)} %param.36) | copy-start | bytes 3076
  7.2 29.5 %all-gather.8.cloned.1.call-start = ((), (), s32[]{:S(2)}) async-start(), calls=%async_computation.7 | async-start | bytes 1327104 | tf_op jit(solution)/shard_map/all_gather | solution.py:86
  7.9 59.7 %all-gather.12.cloned.1.call-start = ((), (), s32[]{:S(2)}) async-start(), calls=%async_computation.9 | async-start | bytes 2654208 | tf_op jit(solution)/shard_map/all_gather | solution.py:85
  8.7 89.4 %all-gather.10.cloned.1.call-start = ((), (), s32[]{:S(2)}) async-start(), calls=%async_computation.8 | async-start | bytes 2359296 | tf_op jit(solution)/shard_map/all_gather | solution.py:103
  9.4 30.3 %copy-start.45 = (f32[1,256]{1,0:T(1,128)}, f32[1,256]{1,0:T(1,128)S(1)}, u32[]{:S(2)}) copy-start(f32[1,256]{1,0:T(1,128)S(1)} %convert_element_type.195) | copy-start | bytes 3076
  9.4 32.1 %copy-start.47 = (f32[128]{0:T(128)}, f32[128]{0:T(128)S(1)}, u32[]{:S(2)}) copy-start(f32[128]{0:T(128)S(1)} %negate_power_fusion) | copy-start | bytes 1540
  10.7 60.0 %copy-start.38 = (f32[256]{0:T(256)}, f32[256]{0:T(256)S(1)}, u32[]{:S(2)}) copy-start(f32[256]{0:T(256)S(1)} %add_rsqrt_fusion.5) | copy-start | bytes 3076
  42.2 86.6 %all-gather.14.cloned.1.call-start = ((), (), s32[]{:S(2)}) async-start(), calls=%async_computation.10 | async-start | bytes 2654208 | tf_op jit(solution)/shard_map/all_gather | solution.py:87
  42.8 174.0 %all-gather.16.cloned.1.call-start = ((), (), s32[]{:S(2)}) async-start(), calls=%async_computation.11 | async-start | bytes 17915904 | tf_op jit(solution)/shard_map/all_gather | solution.py:88
  43.4 261.5 %all-gather.18.cloned.1.call-start = ((), (), s32[]{:S(2)}) async-start(), calls=%async_computation.12 | async-start | bytes 17915904 | tf_op jit(solution)/shard_map/all_gather | solution.py:89
  44.0 349.1 %all-gather.20.cloned.1.call-start = ((), (), s32[]{:S(2)}) async-start(), calls=%async_computation.13 | async-start | bytes 17915904 | tf_op jit(solution)/shard_map/all_gather | solution.py:90
  44.7 467.7 %reduce-scatter.8.cloned.1.call-start = ((), (), s32[]{:S(2)}) async-start(), calls=%async_computation.14 | async-start | bytes 2359296 | tf_op jit(solution)/shard_map/reduce_scatter | solution.py:217
  104.8 26.7 %copy-start.16 = (bf16[256,1024]{1,0:T(8,128)(2,1)}, bf16[256,1024]{1,0:T(8,128)(2,1)S(1)}, u32[]{:S(2)}) copy-start(bf16[256,1024]{1,0:T(8,128)(2,1)S(1)} %convert_element_type.202) | copy-start | bytes 1572868
  104.8 26.7 %copy-start.33 = (f32[1152]{0:T(1024)S(1)}, f32[1152]{0:T(1024)}, u32[]{:S(2)}) copy-start(f32[1152]{0:T(1024)} %param.32) | copy-start | bytes 13828
  132.4 172.5 %copy-start.14 = (bf16[256,1152]{1,0:T(8,128)(2,1)}, bf16[256,1152]{1,0:T(8,128)(2,1)S(1)}, u32[]{:S(2)}) copy-start(bf16[256,1152]{1,0:T(8,128)(2,1)S(1)} %multiply_convert_fusion.4) | copy-start | bytes 1769476
  393.1 10.5 copy-start.8
  393.1 10.5 copy-start.36
  405.2 16.0 %copy-start.21 = (bf16[256,1152]{1,0:T(8,128)(2,1)}, bf16[256,1152]{1,0:T(8,128)(2,1)S(1)}, u32[]{:S(2)}) copy-start(bf16[256,1152]{1,0:T(8,128)(2,1)S(1)} %get-tuple-element.359) | copy-start | bytes 1769476
  421.3 10.5 copy-start.18
  455.9 102.7 %reduce-scatter.10.cloned.1.call-start = ((), (), s32[]{:S(2)}) async-start(), calls=%async_computation.15 | async-start | bytes 2654208 | tf_op jit(solution)/shard_map/reduce_scatter | solution.py:250
  462.6 141.8 %reduce-scatter.14.cloned.1.call-start = ((), (), s32[]{:S(2)}) async-start(), calls=%async_computation.17 | async-start | bytes 2654208 | tf_op jit(solution)/shard_map/reduce_scatter | solution.py:256
  464.9 49.4 %copy-start.46 = (f32[1,256]{1,0:T(1,128)S(1)}, f32[1,256]{1,0:T(1,128)}, u32[]{:S(2)}) copy-start(f32[1,256]{1,0:T(1,128)} %copy-done.45) | copy-start | bytes 3076
  464.9 49.4 %copy-start.48 = (f32[128]{0:T(128)S(1)}, f32[128]{0:T(128)}, u32[]{:S(2)}) copy-start(f32[128]{0:T(128)} %copy-done.47) | copy-start | bytes 1540
  464.9 50.0 %copy-start.20 = (f32[256,512]{1,0:T(8,128)S(1)}, f32[256,512]{1,0:T(8,128)}, u32[]{:S(2)}) copy-start(f32[256,512]{1,0:T(8,128)} %copy-done.19) | copy-start | bytes 1572868
  464.9 50.0 %copy-start.41 = (f32[256]{0:T(256)S(1)}, f32[256]{0:T(256)}, u32[]{:S(2)}) copy-start(f32[256]{0:T(256)} %copy-done.40) | copy-start | bytes 3076
  465.0 50.0 %copy-start.44 = (f32[256]{0:T(256)S(1)}, f32[256]{0:T(256)}, u32[]{:S(2)}) copy-start(f32[256]{0:T(256)} %param.36) | copy-start | bytes 3076
  465.0 179.8 %reduce-scatter.12.cloned.1.call-start = ((), (), s32[]{:S(2)}) async-start(), calls=%async_computation.16 | async-start | bytes 1327104 | tf_op jit(solution)/shard_map/reduce_scatter | solution.py:253
  517.0 244.2 %reduce-scatter.16.cloned.1.call-start = ((), (), s32[]{:S(2)}) async-start(), calls=%async_computation.18 | async-start | bytes 17915904 | tf_op jit(solution)/shard_map/reduce_scatter | solution.py:259
  528.0 350.1 %reduce-scatter.18.cloned.1.call-start = ((), (), s32[]{:S(2)}) async-start(), calls=%async_computation.19 | async-start | bytes 17915904 | tf_op jit(solution)/shard_map/reduce_scatter | solution.py:262
  539.0 455.4 %reduce-scatter.20.cloned.1.call-start = ((), (), s32[]{:S(2)}) async-start(), calls=%async_computation.20 | async-start | bytes 17915904 | tf_op jit(solution)/shard_map/reduce_scatter | solution.py:265
  551.0 684.9 %all-reduce.11.cloned.1.call-start = ((), (), s32[]{:S(2)}) async-start(), calls=%async_computation.21 | async-start | bytes 13418496 | tf_op jit(solution)/shard_map/psum | solution.py:288
  997.5 43.4 %copy-start.7 = (f32[256,1152]{1,0:T(8,128)S(1)}, f32[256,1152]{1,0:T(8,128)}, u32[]{:S(2)}) copy-start(f32[256,1152]{1,0:T(8,128)} %copy-done.6) | copy-start | bytes 3538948
  (33 other events, 62.8 us)
Sparse Core Ops, SparseCore 0:
  9.9 26.7 all-gather.7
  38.6 29.0 all-gather.11
  70.1 27.8 all-gather.9
  99.8 29.0 all-gather.13
  130.6 86.2 all-gather.15
  218.6 86.2 all-gather.17
  306.8 86.2 all-gather.19
  456.1 56.3 reduce-scatter.7
  516.1 42.4 reduce-scatter.9
  561.9 42.4 reduce-scatter.13
  607.9 36.7 reduce-scatter.11
  648.2 112.8 reduce-scatter.15
  765.2 112.8 reduce-scatter.17
  881.6 112.8 reduce-scatter.19
  997.4 238.3 all-reduce.10
where the time goes:
time: 1260 us
  waiting for transfers between devices  1020 us (81%)
  matrix products  134 us (11%)
  blocking collectives  36.7 us (3%)
  other arithmetic  28.9 us (2%)
  local copies, waits for them, and re-layouts  20.3 us (2%)
  between operations  16.2 us (1%)
    psum x1, waiting for transfers between devices, on_device(): lax.psum(grad_queryw.astype(jnp.bfloat16), 'dp').astype(jnp.float32)  194 us
    reduce_scatter x1, waiting for transfers between devices, on_device(): lax.psum_scatter(grad_upw.astype(jnp.bfloat16), 'seq', scatter_dimension=...  117 us
    reduce_scatter x1, waiting for transfers between devices, on_device(): lax.psum_scatter(grad_down.astype(jnp.bfloat16), 'seq', scatter_dimension...  116 us
    reduce_scatter x1, waiting for transfers between devices, on_device(): lax.psum_scatter(grad_gate.astype(jnp.bfloat16), 'seq', scatter_dimension...  116 us
    all_gather x1, waiting for transfers between devices, on_device(): lax.all_gather(w_gate, 'seq', axis=1, tiled=True)  84.5 us
    all_gather x1, waiting for transfers between devices, on_device(): lax.all_gather(w_down, 'seq', axis=0, tiled=True)  75.5 us
    all_gather x1, waiting for transfers between devices, on_device(): lax.all_gather(w_up, 'seq', axis=1, tiled=True)  71.5 us
    reduce_scatter x1, waiting for transfers between devices, on_device(): lax.psum_scatter(d_kv_whole.astype(jnp.bfloat16), 'seq', scatter_dimensio...  47.4 us
  transfers between devices with their start and end apart: 15, of which 15 were waited for; matrix products, arithmetic and copies ran while one was open for 8% of the time, Pallas kernels for 0%

commit v1 on v0

--- a/solution.py
+++ b/solution.py
@@ -285,7 +285,7 @@
         ).astype(jnp.float32),
     )
     totals = (
-        lax.psum(grad_queryw.astype(jnp.bfloat16), "dp").astype(jnp.float32),
+        jnp.sum(lax.all_gather(grad_queryw.astype(jnp.bfloat16), "dp"), axis=0).astype(jnp.float32),
         lax.psum(grad_keyvalw.astype(jnp.bfloat16), "dp").astype(jnp.float32),
         lax.psum(grad_outw.astype(jnp.bfloat16), "dp").astype(jnp.float32),
         lax.psum(grad_gate.astype(jnp.bfloat16), "dp").astype(jnp.float32),

time: 1260 us -> 1280 us (1.016)
  waiting for transfers between devices: 1020 us -> 1040 us
    psum x1, waiting for transfers between devices: 194 us -> 213 us  [on_device(): lax.psum(grad_keyvalw.astype(jnp.bfloat16), 'dp').astype(jnp.float32)]
  transfers between devices with their start and end apart: 15 -> 16, of which waited for: 15 -> 15; matrix products, arithmetic and copies ran while one was open for 8% -> 8% of each run, Pallas kernels for 0% -> 0%
where the time goes in v1:
time: 1280 us
  waiting for transfers between devices  1040 us (81%)
  matrix products  134 us (10%)
  blocking collectives  36.1 us (3%)
  other arithmetic  31 us (2%)
  local copies, waits for them, and re-layouts  20.1 us (2%)
  between operations  16.3 us (1%)
    psum x1, waiting for transfers between devices, on_device(): lax.psum(grad_keyvalw.astype(jnp.bfloat16), 'dp').astype(jnp.float32)  213 us
    reduce_scatter x1, waiting for transfers between devices, on_device(): lax.psum_scatter(grad_upw.astype(jnp.bfloat16), 'seq', scatter_dimension=...  117 us
    reduce_scatter x1, waiting for transfers between devices, on_device(): lax.psum_scatter(grad_gate.astype(jnp.bfloat16), 'seq', scatter_dimension...  116 us
    reduce_scatter x1, waiting for transfers between devices, on_device(): lax.psum_scatter(grad_down.astype(jnp.bfloat16), 'seq', scatter_dimension...  116 us
    all_gather x1, waiting for transfers between devices, on_device(): lax.all_gather(w_gate, 'seq', axis=1, tiled=True)  84.5 us
    all_gather x1, waiting for transfers between devices, on_device(): lax.all_gather(w_down, 'seq', axis=0, tiled=True)  75.5 us
    all_gather x1, waiting for transfers between devices, on_device(): lax.all_gather(w_up, 'seq', axis=1, tiled=True)  71.5 us
    reduce_scatter x1, waiting for transfers between devices, on_device(): lax.psum_scatter(d_kv_whole.astype(jnp.bfloat16), 'seq', scatter_dimensio...  47.4 us
  transfers between devices with their start and end apart: 16, of which 15 were waited for; matrix products, arithmetic and copies ran while one was open for 8% of the time, Pallas kernels for 0%

profile of v1, /device:TPU:0, one launch (start us, length us, event | category | flops | bytes accessed | tf_op | source)
XLA Modules:
  0.0 1275.4 jit_solution(8196220181000438740)
XLA Ops:
  10.7 26.0 %all-gather.10.cloned.1.call-done = bf16[1152,512]{1,0:T(8,128)(2,1)} async-done(((bf16[144,512]{1,0:T(8,128)(2,1)}), bf16[1152,512]{1,0:T(8,128)(2,1)}) %all-gather.10.cloned.1.call-update) | async-done | bytes 1179664 | tf_op jit(solution)/shard_map/all_gather | solution.py:86
  44.8 22.8 %all-gather.14.cloned.1.call-done = bf16[1152,1024]{1,0:T(8,128)(2,1)} async-done(((bf16[144,1024]{1,0:T(8,128)(2,1)}), bf16[1152,1024]{1,0:T(8,128)(2,1)}) %all-gather.14.cloned.1.call-update) | async-done | bytes 2359312 | tf_op jit(solution)/shard_map/all_gather | solution.py:85
  67.6 3.1 copy.39
  73.0 25.0 %all-gather.12.cloned.1.call-done = bf16[2048,512]{1,0:T(8,128)(2,1)} async-done(((bf16[256,512]{1,0:T(8,128)(2,1)}), bf16[2048,512]{1,0:T(8,128)(2,1)}) %all-gather.12.cloned.1.call-update) | async-done | bytes 2097168 | tf_op jit(solution)/shard_map/all_gather | solution.py:103
  98.0 2.9 while.37
  101.0 2.8 while.38
  104.8 24.0 %all-gather.16.cloned.1.call-done = bf16[1024,1152]{1,0:T(8,128)(2,1)} async-done(((bf16[128,1152]{1,0:T(8,128)(2,1)}), bf16[1024,1152]{1,0:T(8,128)(2,1)}) %all-gather.16.cloned.1.call-update) | async-done | bytes 2359312 | tf_op jit(solution)/shard_map/all_gather | solution.py:87
  132.4 84.5 %all-gather.18.cloned.1.call-done = bf16[1152,6912]{0,1:T(8,128)(2,1)} async-done(((bf16[1152,864]{0,1:T(8,128)(2,1)}), bf16[1152,6912]{0,1:T(8,128)(2,1)}) %all-gather.18.cloned.1.call-update) | async-done | bytes 15925264 | tf_op jit(solution)/shard_map/all_gather | solution.py:88
  216.9 16.5 %fusion.84 = f32[256,6912]{1,0:T(8,128)} fusion(bf16[256,1152]{1,0:T(8,128)(2,1)S(1)} %multiply_convert_fusion.4, bf16[1152,6912]{0,1:T(8,128)(2,1)} %all-gather.18.cloned.1.call-done), kind=kOutput, calls=%fused_computation.160 | convolution fusion | flops 4076863488 | bytes 23592960 | tf_op jit(solution)/shard_map/dot_general | solution.py:161
  233.4 71.5 %all-gather.20.cloned.1.call-done = bf16[1152,6912]{0,1:T(8,128)(2,1)} async-done(((bf16[1152,864]{0,1:T(8,128)(2,1)}), bf16[1152,6912]{0,1:T(8,128)(2,1)}) %all-gather.20.cloned.1.call-update) | async-done | bytes 15925264 | tf_op jit(solution)/shard_map/all_gather | solution.py:89
  304.9 12.7 multiply_convert_fusion.1
  317.6 75.5 %all-gather.22.cloned.1.call-done = bf16[6912,1152]{1,0:T(8,128)(2,1)} async-done(((bf16[864,1152]{1,0:T(8,128)(2,1)}), bf16[6912,1152]{1,0:T(8,128)(2,1)}) %all-gather.22.cloned.1.call-update) | async-done | bytes 15925264 | tf_op jit(solution)/shard_map/all_gather | solution.py:90
  393.1 10.5 multiply_reduce_fusion.5
  405.2 16.0 %multiply_convert_fusion = (bf16[256,6912]{1,0:T(8,128)(2,1)}, bf16[256,6912]{1,0:T(8,128)(2,1)}) fusion(f32[256,6912]{1,0:T(8,128)} %fusion.84, f32[256,6912]{1,0:T(8,128)} %get-tuple-element.377, bf16[256,1152]{1,0:T(8,128)(2,1)S(1)} %get-tuple-element.358, bf16[6912,1152]{1,0:T(8,128)(2,1)} %all-gather.22.cloned.1.call-done), kind=kOutput, calls=%fused_computation.60 | convolution fusion | flops 4119330816 | bytes 37748736 | tf_op jit(solution)/shard_map/dot_general | solution.py:43
  421.3 10.5 fusion.85
  431.8 9.5 multiply_reduce_fusion
  448.4 7.5 while.39
  465.0 47.4 %reduce-scatter.8.cloned.1.call-done = bf16[256,512]{1,0:T(8,128)(2,1)} async-done(((bf16[2048,512]{1,0:T(8,128)(2,1)}), bf16[256,512]{1,0:T(8,128)(2,1)}) %reduce-scatter.8.cloned.1.call-update) | async-done | bytes 262160 | tf_op jit(solution)/shard_map/reduce_scatter | solution.py:217
  517.0 11.0 convolution_convert_fusion.2
  528.1 10.9 convolution_convert_fusion.1
  540.1 10.9 convolution_convert_fusion
  551.1 7.6 reduce-scatter.10.cloned.1.call-done
  559.0 45.4 %reduce-scatter.14.cloned.1.call-done = bf16[128,1152]{1,0:T(8,128)(2,1)} async-done(((bf16[1024,1152]{1,0:T(8,128)(2,1)}), bf16[128,1152]{1,0:T(8,128)(2,1)}) %reduce-scatter.14.cloned.1.call-update) | async-done | bytes 294928 | tf_op jit(solution)/shard_map/reduce_scatter | solution.py:256
  604.4 40.4 %reduce-scatter.12.cloned.1.call-done = bf16[144,512]{1,0:T(8,128)(2,1)} async-done(((bf16[1152,512]{1,0:T(8,128)(2,1)}), bf16[144,512]{1,0:T(8,128)(2,1)}) %reduce-scatter.12.cloned.1.call-update) | async-done | bytes 147472 | tf_op jit(solution)/shard_map/reduce_scatter | solution.py:253
  644.7 116.4 %reduce-scatter.16.cloned.1.call-done = bf16[1152,864]{0,1:T(8,128)(2,1)} async-done(((bf16[1152,6912]{0,1:T(8,128)(2,1)}), bf16[1152,864]{0,1:T(8,128)(2,1)}) %reduce-scatter.16.cloned.1.call-update) | async-done | bytes 1990672 | tf_op jit(solution)/shard_map/reduce_scatter | solution.py:259
  761.1 116.9 %reduce-scatter.18.cloned.1.call-done = bf16[1152,864]{0,1:T(8,128)(2,1)} async-done(((bf16[1152,6912]{0,1:T(8,128)(2,1)}), bf16[1152,864]{0,1:T(8,128)(2,1)}) %reduce-scatter.18.cloned.1.call-update) | async-done | bytes 1990672 | tf_op jit(solution)/shard_map/reduce_scatter | solution.py:262
  878.1 116.4 %reduce-scatter.20.cloned.1.call-done = bf16[864,1152]{1,0:T(8,128)(2,1)} async-done(((bf16[6912,1152]{1,0:T(8,128)(2,1)}), bf16[864,1152]{1,0:T(8,128)(2,1)}) %reduce-scatter.20.cloned.1.call-update) | async-done | bytes 1990672 | tf_op jit(solution)/shard_map/reduce_scatter | solution.py:265
  997.5 3.0 fusion.62
  1000.5 24.3 %all-reduce.6 = (bf16[1152]{0:T(1024)(128)(2,1)S(1)}, bf16[1152]{0:T(1024)(128)(2,1)S(1)}, bf16[1152]{0:T(1024)(128)(2,1)S(1)}, bf16[1152]{0:T(1024)(128)(2,1)S(...) all-reduce(bf16[1152]{0:T(1024)(128)(2,1)S(1)} %get-tuple-element.2, ...), channel_id=10, replica_groups=mesh['dp'=4,'seq'=8] {'seq'}, use_global_device_ids=true, to_apply=%region_35.36.clone | all-reduce | flops 5120 | bytes 20480
  1025.2 11.8 all-reduce.7
  1044.0 212.6 %all-reduce.11.cloned.1.call-done = (bf16[144,512]{1,0:T(8,128)(2,1)}, bf16[128,1152]{1,0:T(8,128)(2,1)}, bf16[1152,864]{0,1:T(8,128)(2,1)}, bf16[1152,864]{0,1:T(8,128)(2,1)}, bf16[864,1152]{1,0:T(8,128)(2,1)}) async-done(((bf16[144,512]{1,0:T(8,128)(2,1)}, bf16[128,1152]{1,0:T(8,128)(2,1)}, bf16[1152,864]{0,1:T(8,128)(2,1)}, bf16[1152,864]{0,1:T(8,128)(2,1)}, bf16[864,1152]{1,0:T(8,128)(2,1)}), ...) | async-done | bytes 6414352 | tf_op jit(solution)/shard_map/psum | solution.py:289
  1260.2 3.9 convert_element_type.225
  (245 shorter events, 71.9 us)
Async XLA Ops:
  7.2 32.4 %copy-start.42 = (f32[256]{0:T(256)S(1)}, f32[256]{0:T(256)}, u32[]{:S(2)}) copy-start(f32[256]{0:T(256)} %param.36) | copy-start | bytes 3076
  7.2 29.5 %all-gather.10.cloned.1.call-start = ((), (), s32[]{:S(2)}) async-start(), calls=%async_computation.7 | async-start | bytes 1327104 | tf_op jit(solution)/shard_map/all_gather | solution.py:86
  7.9 59.7 %all-gather.14.cloned.1.call-start = ((), (), s32[]{:S(2)}) async-start(), calls=%async_computation.9 | async-start | bytes 2654208 | tf_op jit(solution)/shard_map/all_gather | solution.py:85
  8.7 89.4 %all-gather.12.cloned.1.call-start = ((), (), s32[]{:S(2)}) async-start(), calls=%async_computation.8 | async-start | bytes 2359296 | tf_op jit(solution)/shard_map/all_gather | solution.py:103
  9.4 30.3 %copy-start.44 = (f32[1,256]{1,0:T(1,128)}, f32[1,256]{1,0:T(1,128)S(1)}, u32[]{:S(2)}) copy-start(f32[1,256]{1,0:T(1,128)S(1)} %convert_element_type.197) | copy-start | bytes 3076
  9.4 32.0 %copy-start.46 = (f32[128]{0:T(128)}, f32[128]{0:T(128)S(1)}, u32[]{:S(2)}) copy-start(f32[128]{0:T(128)S(1)} %negate_power_fusion) | copy-start | bytes 1540
  10.7 60.0 %copy-start.37 = (f32[256]{0:T(256)}, f32[256]{0:T(256)S(1)}, u32[]{:S(2)}) copy-start(f32[256]{0:T(256)S(1)} %add_rsqrt_fusion.5) | copy-start | bytes 3076
  42.2 86.6 %all-gather.16.cloned.1.call-start = ((), (), s32[]{:S(2)}) async-start(), calls=%async_computation.10 | async-start | bytes 2654208 | tf_op jit(solution)/shard_map/all_gather | solution.py:87
  42.8 174.1 %all-gather.18.cloned.1.call-start = ((), (), s32[]{:S(2)}) async-start(), calls=%async_computation.11 | async-start | bytes 17915904 | tf_op jit(solution)/shard_map/all_gather | solution.py:88
  43.4 261.5 %all-gather.20.cloned.1.call-start = ((), (), s32[]{:S(2)}) async-start(), calls=%async_computation.12 | async-start | bytes 17915904 | tf_op jit(solution)/shard_map/all_gather | solution.py:89
  44.0 349.1 %all-gather.22.cloned.1.call-start = ((), (), s32[]{:S(2)}) async-start(), calls=%async_computation.13 | async-start | bytes 17915904 | tf_op jit(solution)/shard_map/all_gather | solution.py:90
  44.7 467.7 %reduce-scatter.8.cloned.1.call-start = ((), (), s32[]{:S(2)}) async-start(), calls=%async_computation.14 | async-start | bytes 2359296 | tf_op jit(solution)/shard_map/reduce_scatter | solution.py:217
  104.8 26.7 %copy-start.16 = (bf16[256,1024]{1,0:T(8,128)(2,1)}, bf16[256,1024]{1,0:T(8,128)(2,1)S(1)}, u32[]{:S(2)}) copy-start(bf16[256,1024]{1,0:T(8,128)(2,1)S(1)} %convert_element_type.204) | copy-start | bytes 1572868
  104.8 26.7 %copy-start.32 = (f32[1152]{0:T(1024)S(1)}, f32[1152]{0:T(1024)}, u32[]{:S(2)}) copy-start(f32[1152]{0:T(1024)} %param.32) | copy-start | bytes 13828
  132.4 172.5 %copy-start.14 = (bf16[256,1152]{1,0:T(8,128)(2,1)}, bf16[256,1152]{1,0:T(8,128)(2,1)S(1)}, u32[]{:S(2)}) copy-start(bf16[256,1152]{1,0:T(8,128)(2,1)S(1)} %multiply_convert_fusion.4) | copy-start | bytes 1769476
  393.1 10.5 copy-start.35
  405.2 16.1 %copy-start.21 = (bf16[256,1152]{1,0:T(8,128)(2,1)}, bf16[256,1152]{1,0:T(8,128)(2,1)S(1)}, u32[]{:S(2)}) copy-start(bf16[256,1152]{1,0:T(8,128)(2,1)S(1)} %get-tuple-element.358) | copy-start | bytes 1769476
  421.3 10.5 copy-start.18
  456.0 102.7 %reduce-scatter.10.cloned.1.call-start = ((), (), s32[]{:S(2)}) async-start(), calls=%async_computation.15 | async-start | bytes 2654208 | tf_op jit(solution)/shard_map/reduce_scatter | solution.py:250
  462.6 141.8 %reduce-scatter.14.cloned.1.call-start = ((), (), s32[]{:S(2)}) async-start(), calls=%async_computation.17 | async-start | bytes 2654208 | tf_op jit(solution)/shard_map/reduce_scatter | solution.py:256
  464.9 49.4 %copy-start.45 = (f32[1,256]{1,0:T(1,128)S(1)}, f32[1,256]{1,0:T(1,128)}, u32[]{:S(2)}) copy-start(f32[1,256]{1,0:T(1,128)} %copy-done.44) | copy-start | bytes 3076
  464.9 49.4 %copy-start.47 = (f32[128]{0:T(128)S(1)}, f32[128]{0:T(128)}, u32[]{:S(2)}) copy-start(f32[128]{0:T(128)} %copy-done.46) | copy-start | bytes 1540
  464.9 50.0 %copy-start.20 = (f32[256,512]{1,0:T(8,128)S(1)}, f32[256,512]{1,0:T(8,128)}, u32[]{:S(2)}) copy-start(f32[256,512]{1,0:T(8,128)} %copy-done.19) | copy-start | bytes 1572868
  464.9 50.0 %copy-start.40 = (f32[256]{0:T(256)S(1)}, f32[256]{0:T(256)}, u32[]{:S(2)}) copy-start(f32[256]{0:T(256)} %copy-done.39) | copy-start | bytes 3076
  464.9 50.0 %copy-start.43 = (f32[256]{0:T(256)S(1)}, f32[256]{0:T(256)}, u32[]{:S(2)}) copy-start(f32[256]{0:T(256)} %param.36) | copy-start | bytes 3076
  465.0 179.8 %reduce-scatter.12.cloned.1.call-start = ((), (), s32[]{:S(2)}) async-start(), calls=%async_computation.16 | async-start | bytes 1327104 | tf_op jit(solution)/shard_map/reduce_scatter | solution.py:253
  517.0 244.2 %reduce-scatter.16.cloned.1.call-start = ((), (), s32[]{:S(2)}) async-start(), calls=%async_computation.18 | async-start | bytes 17915904 | tf_op jit(solution)/shard_map/reduce_scatter | solution.py:259
  528.1 350.0 %reduce-scatter.18.cloned.1.call-start = ((), (), s32[]{:S(2)}) async-start(), calls=%async_computation.19 | async-start | bytes 17915904 | tf_op jit(solution)/shard_map/reduce_scatter | solution.py:262
  539.1 455.4 %reduce-scatter.20.cloned.1.call-start = ((), (), s32[]{:S(2)}) async-start(), calls=%async_computation.20 | async-start | bytes 17915904 | tf_op jit(solution)/shard_map/reduce_scatter | solution.py:265
  551.0 490.6 %all-gather.24.cloned.1.call-start = ((), (), s32[]{:S(2)}) async-start(), calls=%async_computation.21 | async-start | bytes 1474560 | tf_op jit(solution)/shard_map/all_gather | solution.py:288
  558.7 698.0 %all-reduce.11.cloned.1.call-start = ((), (), s32[]{:S(2)}) async-start(), calls=%async_computation.22 | async-start | bytes 12828672 | tf_op jit(solution)/shard_map/psum | solution.py:289
  997.5 42.8 %copy-start.7 = (f32[256,1152]{1,0:T(8,128)S(1)}, f32[256,1152]{1,0:T(8,128)}, u32[]{:S(2)}) copy-start(f32[256,1152]{1,0:T(8,128)} %copy-done.6) | copy-start | bytes 3538948
  (33 other events, 69.3 us)
Sparse Core Ops, SparseCore 0:
  9.9 26.7 all-gather.9
  38.6 29.0 all-gather.13
  70.1 27.8 all-gather.11
  99.8 29.0 all-gather.15
  130.6 86.2 all-gather.17
  218.6 86.2 all-gather.19
  306.8 86.2 all-gather.21
  456.1 56.3 reduce-scatter.7
  516.2 42.4 reduce-scatter.9
  561.9 42.4 reduce-scatter.13
  608.0 36.7 reduce-scatter.11
  648.2 112.8 reduce-scatter.15
  765.2 112.8 reduce-scatter.17
  881.6 112.8 reduce-scatter.19
  995.9 30.4 all-gather.23
  1029.3 227.3 all-reduce.10
